TPU v7x, 32 devices: a whole 2x2x4 slice. The times are simulated.
32 devices in a mesh: group: 2 (over x), loop: 16 (over z, y, core).
Axes of the slice: x: 2, y: 2, z: 4, core: 2. Of those that a mesh axis runs over, the one named last changes fastest.
Arguments:
- users: float32 [8192, 512], P(('group', 'loop')), parts along dimension 0, may hold values from -1.3 to 1.3
- items: bfloat16 [4096, 512], P(('group', 'loop')), parts along dimension 0, may hold values from -1.296875 to 1.296875
- tile_blocks: int32 [32, 8], P(('group', 'loop')), parts along dimension 0, may hold values from 0 to 15, as said below
- tile_count: int32 [32], P(('group', 'loop')), parts along dimension 0, may hold values from 1 to 8, as said below
- labels: int32 [8192, 1024], P(('group', 'loop')), parts along dimension 0, may hold values 0 or 1
Outputs:
- new_users: float32 [8192, 512], P(('group', 'loop')), parts along dimension 0
There are 2 independent parts, one for each index of `group`. A program takes and returns all parts, laid end to end along the dimension named above; each array names one. Nothing has to cross between parts.
Inputs may be any that keep to these rules, and one draw needn't show every extreme that they name: `tile_blocks`: in each row the entries are distinct item blocks; only the first tile_count of them are used. `tile_count`: some user block has all 8 tiles live.
All inputs are finite; a program needn't handle non-finite values. No bound on the sum of `labels` on one device may be relied on, other than what follows from the above.
Results may differ from a plain program's by a relative error of at most 0.0003.
Values may be sent and summed in bfloat16 or wider, within the bound.
A program may use at most 64 MiB of HBM per device.

v0:
```python
import jax
import jax.numpy as jnp
from jax import lax
from jax.sharding import PartitionSpec as P


def slot_table(block_list, live_count, lowest, loop_size):
    slot_ids = jnp.arange(block_list.shape[0], dtype=jnp.int32)
    block_ids = jnp.arange(loop_size, dtype=jnp.int32)
    usable = (slot_ids >= lowest) & (slot_ids < live_count)
    matches = (block_list[None, :] == block_ids[:, None]) & usable[None, :]
    return jnp.sum(jnp.where(matches, slot_ids[None, :] + 1, 0), axis=1) - 1


def score_tile(user_rows, item_block):
    return jnp.dot(
        user_rows, item_block.T, precision=lax.Precision.HIGHEST, preferred_element_type=jnp.float32
    )


def apply_tile(weights, item_block):
    return jnp.dot(
        weights, item_block, precision=lax.Precision.HIGHEST, preferred_element_type=jnp.float32
    )


def label_slice(labels, slot_index, tile_width):
    return lax.dynamic_slice_in_dim(labels, slot_index * tile_width, tile_width, 1).astype(
        jnp.float32
    )


def take_block(piece, index, tile_width):
    return lax.dynamic_slice_in_dim(piece, index * tile_width, tile_width, 0).astype(jnp.float32)


def local(users, items, tile_blocks, tile_count, labels):
    tile_width = items.shape[0]
    loop_size = lax.axis_size("loop")
    block_list = tile_blocks[0]
    live_count = tile_count[0]
    zero_grad = jnp.zeros(users.shape, jnp.float32)
    own_slots = slot_table(block_list, live_count, 0, loop_size)
    piece = lax.all_gather(items, "loop", axis=0, tiled=True)

    def sweep_blocks(index, current):
        item_block = take_block(piece, index, tile_width)
        own_index = own_slots[index]

        def full_work(values):
            residual = jax.nn.sigmoid(score_tile(users, item_block)) - label_slice(
                labels, own_index, tile_width
            )
            return values + apply_tile(residual, item_block)

        return lax.cond(own_index >= 0, full_work, lambda values: values, current)

    gradient = lax.fori_loop(0, piece.shape[0] // tile_width, sweep_blocks, zero_grad)
    squares = lax.psum(jnp.sum(gradient * gradient), "loop")
    entries = users.shape[0] * loop_size * users.shape[1]
    grad_rms = jnp.sqrt(squares / entries + 1e-06)
    step_scale = 0.5 / grad_rms
    return users - step_scale * gradient


def solution(mesh):
    in_specs = (
        P(("group", "loop"), None),
        P(("group", "loop"), None),
        P(("group", "loop"), None),
        P(("group", "loop")),
        P(("group", "loop"), None),
    )
    out_specs = P(("group", "loop"), None)
    return jax.shard_map(local, mesh=mesh, in_specs=in_specs, out_specs=out_specs, check_vma=False)
```

profile of v0, /device:TPU:0, one launch (start us, length us, event | category | flops | bytes accessed | tf_op | source)
XLA Modules:
  0.0 153.0 jit_solution(4210043578784997191)
XLA Ops:
  8.7 45.0 %all-gather.2.cloned.1.call-done = bf16[2048,512]{1,0:T(8,128)(2,1)} async-done(((bf16[128,512]{1,0:T(8,128)(2,1)}), bf16[2048,512]{1,0:T(8,128)(2,1)}) %all-gather.2.cloned.1.call-update) | async-done | bytes 2097168 | tf_op jit(solution)/shard_map/all_gather | solution.py:44
  53.7 46.9 %while.16 = (s32[]{:T(128)}, f32[256,512]{1,0:T(8,128)S(1)}, s32[16]{0:T(128)S(1)}, bf16[2048,512]{1,0:T(8,128)(2,1)}, f32[256,512]{1,0:T(8,128)}, /*index=5*/s3...) while((s32[]{:T(128)}, f32[256,512]{1,0:T(8,128)S(1)}, s32[16]{0:T(128)S(1)}, ...), condition=%wide.region_4.5_spmd, body=%wide.region_1.4_spmd.sunk | while | flops 403013632 | bytes 2883867 | solution.py:58
  55.0 0.9 dynamic-slice_convert_fusion.2
  57.2 0.9 dynamic-slice_convert_fusion.2
  59.4 0.9 dynamic-slice_convert_fusion.2
  60.3 3.0 %conditional.2 = (f32[256,512]{1,0:T(8,128)S(1)}) conditional(s32[]{:T(128)} %convert_element_type.22, f32[256,512]{1,0:T(8,128)S(1)} %get-tuple-element.198, (f32[256,512]{1,0:T(8,128)}, f32[128,512]{1,0:T(8,128)S(1)}, s32[]{:T(128)}, s32[256,1024]{1,0:T(8,128)}, f32[256,512]{1,0:T(8,128)S(1)}) %tuple.39), branch_computations={%region_2.2_spmd, %region_3.3_spmd} | conditional | flops 402948096 | bytes 2490426 | solution.py:56
  60.9 1.7 %fusion.3 = f32[256,128]{1,0:T(8,128)S(1)} fusion(f32[256,512]{1,0:T(8,128)} %get-tuple-element.125, f32[128,512]{1,0:T(8,128)S(1)} %get-tuple-element.126, s32[256,1024]{1,0:T(8,128)} %get-tuple-element.127, s32[]{:T(128)S(6)} %select_n.16), kind=kOutput, calls=%fused_computation.5 | convolution fusion | flops 201490432 | bytes 1048580 | tf_op jit(solution)/shard_map/while/body/eval_jaxpr/cond/branch_1_fun/dot_general | solution.py:16
  64.5 0.9 dynamic-slice_convert_fusion.2
  66.7 0.9 dynamic-slice_convert_fusion.2
  68.9 0.9 dynamic-slice_convert_fusion.2
  71.1 0.9 dynamic-slice_convert_fusion.2
  72.0 3.0 %conditional.2 = (f32[256,512]{1,0:T(8,128)S(1)}) conditional(s32[]{:T(128)} %convert_element_type.22, f32[256,512]{1,0:T(8,128)S(1)} %get-tuple-element.198, (f32[256,512]{1,0:T(8,128)}, f32[128,512]{1,0:T(8,128)S(1)}, s32[]{:T(128)}, s32[256,1024]{1,0:T(8,128)}, f32[256,512]{1,0:T(8,128)S(1)}) %tuple.39), branch_computations={%region_2.2_spmd, %region_3.3_spmd} | conditional | flops 402948096 | bytes 2490426 | solution.py:56
  72.7 1.7 %fusion.3 = f32[256,128]{1,0:T(8,128)S(1)} fusion(f32[256,512]{1,0:T(8,128)} %get-tuple-element.125, f32[128,512]{1,0:T(8,128)S(1)} %get-tuple-element.126, s32[256,1024]{1,0:T(8,128)} %get-tuple-element.127, s32[]{:T(128)S(6)} %select_n.16), kind=kOutput, calls=%fused_computation.5 | convolution fusion | flops 201490432 | bytes 1048580 | tf_op jit(solution)/shard_map/while/body/eval_jaxpr/cond/branch_1_fun/dot_general | solution.py:16
  76.2 0.9 dynamic-slice_convert_fusion.2
  78.4 0.9 dynamic-slice_convert_fusion.2
  80.6 0.9 dynamic-slice_convert_fusion.2
  82.8 0.9 dynamic-slice_convert_fusion.2
  85.0 0.9 dynamic-slice_convert_fusion.2
  88.2 2.9 %conditional.2 = (f32[256,512]{1,0:T(8,128)S(1)}) conditional(s32[]{:T(128)} %convert_element_type.22, f32[256,512]{1,0:T(8,128)S(1)} %get-tuple-element.198, (f32[256,512]{1,0:T(8,128)}, f32[128,512]{1,0:T(8,128)S(1)}, s32[]{:T(128)}, s32[256,1024]{1,0:T(8,128)}, f32[256,512]{1,0:T(8,128)S(1)}) %tuple.39), branch_computations={%region_2.2_spmd, %region_3.3_spmd} | conditional | flops 402948096 | bytes 2490426 | solution.py:56
  88.8 1.7 %fusion.3 = f32[256,128]{1,0:T(8,128)S(1)} fusion(f32[256,512]{1,0:T(8,128)} %get-tuple-element.125, f32[128,512]{1,0:T(8,128)S(1)} %get-tuple-element.126, s32[256,1024]{1,0:T(8,128)} %get-tuple-element.127, s32[]{:T(128)S(6)} %select_n.16), kind=kOutput, calls=%fused_computation.5 | convolution fusion | flops 201490432 | bytes 1048580 | tf_op jit(solution)/shard_map/while/body/eval_jaxpr/cond/branch_1_fun/dot_general | solution.py:16
  93.3 2.9 %conditional.2 = (f32[256,512]{1,0:T(8,128)S(1)}) conditional(s32[]{:T(128)} %convert_element_type.22, f32[256,512]{1,0:T(8,128)S(1)} %get-tuple-element.198, (f32[256,512]{1,0:T(8,128)}, f32[128,512]{1,0:T(8,128)S(1)}, s32[]{:T(128)}, s32[256,1024]{1,0:T(8,128)}, f32[256,512]{1,0:T(8,128)S(1)}) %tuple.39), branch_computations={%region_2.2_spmd, %region_3.3_spmd} | conditional | flops 402948096 | bytes 2490426 | solution.py:56
  93.9 1.7 %fusion.3 = f32[256,128]{1,0:T(8,128)S(1)} fusion(f32[256,512]{1,0:T(8,128)} %get-tuple-element.125, f32[128,512]{1,0:T(8,128)S(1)} %get-tuple-element.126, s32[256,1024]{1,0:T(8,128)} %get-tuple-element.127, s32[]{:T(128)S(6)} %select_n.16), kind=kOutput, calls=%fused_computation.5 | convolution fusion | flops 201490432 | bytes 1048580 | tf_op jit(solution)/shard_map/while/body/eval_jaxpr/cond/branch_1_fun/dot_general | solution.py:16
  101.4 42.1 %psum.7 = f32[]{:T(128)} all-reduce(f32[]{:T(128)} %multiply_reduce_fusion), channel_id=1, replica_groups=mesh['group'=2,'loop'=16] {'loop'}, use_global_device_ids=true, to_apply=%region_6.7 | all-reduce | flops 1 | bytes 8 | tf_op jit(solution)/shard_map/psum | solution.py:59
  144.2 1.9 %multiply_subtract_fusion = f32[256,512]{1,0:T(8,128)} fusion(f32[256,512]{1,0:T(8,128)} %get-tuple-element.219, f32[256,512]{1,0:T(8,128)S(1)} %get-tuple-element.137, f32[]{:T(128)S(6)} %div.10), kind=kLoop, calls=%fused_computation.7 | loop fusion | flops 262144 | bytes 1572868 | tf_op jit(solution)/shard_map/sub | solution.py:63
  (44 shorter events, 18.3 us)
Async XLA Ops:
  6.5 47.1 %all-gather.2.cloned.1.call-start = ((), (), s32[]{:S(2)}) async-start(), calls=%async_computation | async-start | bytes 2228224 | tf_op jit(solution)/shard_map/all_gather | solution.py:44
Sparse Core Ops, SparseCore 0:
  9.5 44.0 all-gather.1
where the time goes:
time: 154 us; the launch traced here: 153 us
  waiting for transfers between devices  45.7 us (30%)
  blocking collectives  42.1 us (27%)
  other arithmetic  18.3 us (12%)
  between operations  14.8 us (10%)
  loops' own time  13.3 us (9%)
  local copies, waits for them, and re-layouts  9.56 us (6%)
  matrix products  9.21 us (6%)
    all_gather x1, waiting for transfers between devices, local(): piece = lax.all_gather(items, 'loop', axis=0, tiled=True)  45 us
    psum x1, blocking collectives, local(): squares = lax.psum(jnp.sum(gradient * gradient), 'loop')  42.1 us
    convert_element_type x16, other arithmetic, take_block(): lax.dynamic_slice_in_dim(piece, index * tile_width, tile_width, 0)  14.9 us
    another operation x1, loops' own time, local(): lax.fori_loop(0, piece.shape[0] // tile_width, sweep_blocks, zero_grad)  10.5 us
    dynamic_slice x16, local copies, waits for them, and re-layouts, sweep_blocks(): own_index = own_slots[index]  9.51 us
    dot_general x4, matrix products, score_tile(): jnp.dot(user_rows, item_block.T, precision=lax.Precision.HIGHEST, preferr...  6.64 us
  transfers between devices with their start and end apart: 1, of which 1 were waited for; matrix products, arithmetic and copies ran while one was open for 0% of the time, Pallas kernels for 0%

commit v1 on v0

v1 whole, which is shorter than its diff:
```python
import functools

import jax
import jax.numpy as jnp
from jax import lax
from jax.experimental import pallas as pl
from jax.experimental.pallas import tpu as pltpu
from jax.sharding import PartitionSpec as P

MESH = pl.DeviceIdType.MESH


def grid_of(chips):
    inner = 1
    while (2 * inner) * (2 * inner) <= chips:
        inner *= 2
    return chips // inner, inner


def chip_at(pos, outer, inner):
    wide = inner - 1
    back = lax.div(pos, outer * wide)
    row = lax.div(pos, wide)
    step = lax.rem(pos, wide)
    odd = lax.rem(row, 2)
    column = 1 + step + odd * (wide - 1 - 2 * step)
    there = row * inner + column
    home = (outer - 1 - (pos - outer * wide)) * inner
    return back * home + (1 - back) * there


def place_of(chip, outer, inner):
    wide = inner - 1
    row = lax.div(chip, inner)
    column = lax.rem(chip, inner)
    there = lax.div(column + wide, inner)
    odd = lax.rem(row, 2)
    out = row * wide + column - 1 + odd * (wide + 1 - 2 * column)
    home = outer * wide + outer - 1 - row
    return there * out + (1 - there) * home


def kernel(n, chunks, users_hbm, items_hbm, blocks_ref, count_ref, labels_hbm, grad_hbm, scale_ref,
           users, labels, held, split, grad, mine, parts,
           load_sem, label_sem, ring_send, ring_recv, pair_send, pair_recv, own_sem, sum_sem, store_sem):
    chips = n // 2
    half = chips // 2
    outer, inner = grid_of(chips)
    depth = items_hbm.shape[0]
    height = users_hbm.shape[0]
    slots = blocks_ref.shape[1]
    piece = depth // chunks
    me = lax.axis_index("loop")
    core = lax.rem(me, 2)
    partner = me + 1 - 2 * core
    pos = place_of(lax.div(me, 2), outer, inner)

    def chip_near(offset):
        return chip_at(lax.rem(pos + offset + chips, chips), outer, inner)

    ahead = chip_near(1) * 2 + core
    behind = chip_near(-1) * 2 + core

    def rows_of(block, j):
        return pl.ds(pl.multiple_of(block * depth + j * piece, piece), piece)

    own_rows = pl.ds(pl.multiple_of(me * depth, depth), depth)
    load_items = pltpu.make_async_copy(items_hbm, held.at[own_rows], load_sem.at[0])
    load_users = pltpu.make_async_copy(users_hbm, users, load_sem.at[1])

    def load_labels(s):
        columns = pl.ds(pl.multiple_of(s * depth, depth), depth)
        return pltpu.make_async_copy(labels_hbm.at[:, columns], labels.at[s], label_sem.at[s])

    load_items.start()
    load_users.start()
    for s in range(slots):
        load_labels(s).start()

    barrier = pltpu.get_barrier_semaphore()
    for other in (ahead, behind, partner):
        pl.semaphore_signal(barrier, inc=1, device_id={"loop": other}, device_id_type=MESH)
    pl.semaphore_wait(barrier, 3)
    load_items.wait()

    def chip_of(d, s):
        return chip_near(s * (2 * d - 1))

    def ring_copy(d, hop, j, source):
        block = chip_of(d, source) * 2 + core
        spot = held.at[rows_of(block, j)]
        return pltpu.make_async_remote_copy(
            src_ref=spot, dst_ref=spot,
            send_sem=ring_send.at[d, hop - 1, j], recv_sem=ring_recv.at[d, hop - 1, j],
            device_id={"loop": behind if d else ahead}, device_id_type=MESH)

    def pair_copy(d, s, j, whose):
        block = chip_of(d, s) * 2 + whose
        spot = held.at[rows_of(block, j)]
        return pltpu.make_async_remote_copy(
            src_ref=spot, dst_ref=spot,
            send_sem=pair_send.at[d, s - 1, j], recv_sem=pair_recv.at[d, s - 1, j],
            device_id={"loop": partner}, device_id_type=MESH)

    def own_copy(whose):
        spot = held.at[pl.ds(pl.multiple_of(whose * depth, depth), depth)]
        return pltpu.make_async_remote_copy(
            src_ref=spot, dst_ref=spot, send_sem=own_sem.at[0], recv_sem=own_sem.at[1],
            device_id={"loop": partner}, device_id_type=MESH)

    def shared(d):
        return range(chunks // 2) if d == 0 else range(chunks // 2, chunks)

    order = [(d, j if d == 0 else chunks - 1 - j) for j in range(chunks) for d in (0, 1)]
    last = [(d, j) for d, j in order if j in shared(d)]

    for d, j in order:
        ring_copy(d, 1, j, 0).start()
    own_copy(me).start()

    load_users.wait()
    high = users[...].astype(jnp.bfloat16)
    split[0:height] = high
    split[height:] = (users[...] - high.astype(jnp.float32)).astype(jnp.bfloat16)
    for s in range(slots):
        load_labels(s).wait()
    count = count_ref[0]

    def slot_of(block):
        found = jnp.int32(0)
        for s in range(slots):
            gap = blocks_ref[0, s] - block
            hit = 1 - lax.min(gap * gap, jnp.int32(1))
            used = lax.min(lax.max(count - s, jnp.int32(0)), jnp.int32(1))
            found = found + hit * used * (s + 1)
        return found

    def target_of(block):
        found = slot_of(block)
        slot = lax.max(found - 1, jnp.int32(0))
        live = lax.min(found, jnp.int32(1)).astype(jnp.float32)
        label = labels[slot].astype(jnp.float32)
        return label, live

    def compute(chip, first=False):
        item = held[pl.ds(pl.multiple_of(chip * 2 * depth, 2 * depth), 2 * depth), :]
        both = lax.dot_general(split[...], item, (((1,), (1,)), ((), ())),
                               preferred_element_type=jnp.float32)
        scores = both[:height] + both[height:]
        guess = 0.5 + 0.5 * jnp.tanh(0.5 * scores)
        label0, live0 = target_of(chip * 2)
        label1, live1 = target_of(chip * 2 + 1)
        residual = jnp.concatenate(
            [(guess[:, :depth] - label0) * live0, (guess[:, depth:] - label1) * live1], axis=1)
        top = residual.astype(jnp.bfloat16)
        rest = (residual - top.astype(jnp.float32)).astype(jnp.bfloat16)
        term = (jnp.dot(top, item, preferred_element_type=jnp.float32)
                + jnp.dot(rest, item, preferred_element_type=jnp.float32))
        grad[...] = term if first else grad[...] + term

    def take_pair(d, s, js):
        for j in js:
            pair_copy(d, s, j, 1 - core).wait_recv()

    def arrive(s, d, j, onward):
        ring_copy(d, s, j, s).wait_recv()
        if onward:
            ring_copy(d, s + 1, j, s).start()
        pair_copy(d, s, j, core).start()

    def own_pair():
        own_copy(partner).wait_recv()
        compute(lax.div(me, 2), first=True)

    def earlier(s, d):
        take_pair(d, s, range(chunks))
        compute(chip_of(d, s))

    def full_step(s, final, start):
        for i, (d, j) in enumerate(order):
            arrive(s, d, j, (d, j) in last if final else True)
            if start:
                if i == len(order) // 2 - 1:
                    own_pair()
            else:
                if i == len(order) // 2 - 1:
                    earlier(s - 1, 0)
                if i == len(order) - 1:
                    earlier(s - 1, 1)

    full_step(1, half == 2, True)
    if half <= 4:
        for s in range(2, half - 1):
            full_step(s, False, False)
    else:
        lax.fori_loop(2, half - 1, lambda s, c: (full_step(s, False, False), c)[1], 0)
    if half > 2:
        full_step(half - 1, True, False)
    for d, j in last:
        arrive(half, d, j, False)
    earlier(half - 1, 0)
    earlier(half - 1, 1)
    for d in (0, 1):
        take_pair(d, half, shared(d))
    compute(chip_of(0, half))

    squares = grad[...] * grad[...]
    lanes = 128
    total = squares[:, 0:lanes]
    for k in range(1, squares.shape[1] // lanes):
        total = total + squares[:, k * lanes:(k + 1) * lanes]
    total = jnp.sum(total.reshape(height // 8, 8, lanes), axis=0)
    mine[...] = total

    def sum_copy(k):
        return pltpu.make_async_remote_copy(
            src_ref=mine, dst_ref=parts.at[n - 1 - k], send_sem=sum_sem.at[0], recv_sem=sum_sem.at[1],
            device_id={"loop": lax.rem(me + k, n)}, device_id_type=MESH)

    if n <= 16:
        for k in range(1, n):
            sum_copy(k).start()
    else:
        lax.fori_loop(1, n, lambda k, c: (sum_copy(k).start(), c)[1], 0)
    store = pltpu.make_async_copy(grad, grad_hbm, store_sem)
    store.start()

    own_copy(me).wait_send()

    def drain(s, pairs, ring):
        for d, j in pairs:
            pair_copy(d, s, j, core).wait_send()
        for d, j in ring:
            ring_copy(d, s, j, s - 1).wait_send()

    if half <= 4:
        for s in range(1, half):
            drain(s, order, order)
    else:
        lax.fori_loop(1, half, lambda s, c: (drain(s, order, order), c)[1], 0)
    drain(half, last, last)
    store.wait()

    pltpu.make_async_copy(parts, parts, sum_sem.at[1]).wait()
    pltpu.make_async_copy(parts, parts, sum_sem.at[0]).wait()
    whole = total + jnp.sum(parts[...], axis=0)
    whole = jnp.sum(jnp.sum(whole, axis=1, keepdims=True), axis=0, keepdims=True)
    entries = height * n * users_hbm.shape[1]
    rms = jnp.sqrt(whole / entries + 1e-06)
    scale_ref[...] = jnp.broadcast_to(0.5 / rms, scale_ref.shape)


def solution(mesh):
    n = mesh.shape["loop"]

    def local(users, items, tile_blocks, tile_count, labels):
        height, width = users.shape
        depth = items.shape[0]
        half = n // 4
        chunks = 4 if half <= 4 else 2
        dma = pltpu.SemaphoreType.DMA
        anywhere = pl.BlockSpec(memory_space=pl.ANY)
        scalars = pl.BlockSpec(memory_space=pltpu.SMEM)
        gradient, scale = pl.pallas_call(
            functools.partial(kernel, n, chunks),
            out_shape=(jax.ShapeDtypeStruct((height, width), jnp.float32),
                       jax.ShapeDtypeStruct((8, 128), jnp.float32)),
            in_specs=[anywhere, anywhere, scalars, scalars, anywhere],
            out_specs=(anywhere, pl.BlockSpec(memory_space=pltpu.VMEM)),
            scratch_shapes=[
                pltpu.VMEM((height, width), jnp.float32),
                pltpu.VMEM((tile_blocks.shape[1], height, depth), jnp.int32),
                pltpu.VMEM((n * depth, width), jnp.bfloat16),
                pltpu.VMEM((2 * height, width), jnp.bfloat16),
                pltpu.VMEM((height, width), jnp.float32),
                pltpu.VMEM((8, 128), jnp.float32),
                pltpu.VMEM((n - 1, 8, 128), jnp.float32),
                dma((2,)),
                dma((tile_blocks.shape[1],)),
                dma((2, half, chunks)),
                dma((2, half, chunks)),
                dma((2, half, chunks)),
                dma((2, half, chunks)),
                dma((2,)),
                dma((2,)),
                dma(()),
            ],
            compiler_params=pltpu.CompilerParams(
                collective_id=0, has_side_effects=True, vmem_limit_bytes=60 * 1024 * 1024),
            name="gather_gradient",
        )(users, items, tile_blocks, tile_count, labels)
        return users - scale[0, 0] * gradient

    rows = P(("group", "loop"), None)
    return jax.shard_map(local, mesh=mesh, in_specs=(rows, rows, rows, P(("group", "loop")), rows),
                         out_specs=rows, check_vma=False)
```

time: 154 us -> 31.7 us (0.21)
  waiting for transfers between devices: 45.7 us -> 0 us
  blocking collectives: 42.1 us -> 0 us
  Pallas kernels: 0 us -> 27.1 us
  other arithmetic: 18.3 us -> 2.53 us
  between operations: 14.8 us -> 0.67 us
  loops' own time: 13.3 us -> 0 us
  matrix products: 9.21 us -> 0 us
  local copies, waits for them, and re-layouts: 9.56 us -> 1.23 us
    all_gather x1 -> x0, waiting for transfers between devices: 45 us -> none  [local(): piece = lax.all_gather(items, 'loop', axis=0, tiled=True)]
    psum x1 -> x0, blocking collectives: 42.1 us -> none  [local(): squares = lax.psum(jnp.sum(gradient * gradient), 'loop')]
    pallas_call x0 -> x1, Pallas kernels: none -> 27.1 us  [local(): pl.pallas_call(functools.partial(kernel, n, chunks), out_shape=(jax.Shape...]
    convert_element_type x16 -> x0, other arithmetic: 14.9 us -> none  [take_block(): lax.dynamic_slice_in_dim(piece, index * tile_width, tile_width, 0)]
    another operation x17 -> x0, loops' own time: 13.3 us -> none  [the longest x1 10.5 us: local(): lax.fori_loop(0, piece.shape[0] // tile_width, sweep_blocks, zero_grad)]
    dynamic_slice x16 -> x0, local copies, waits for them, and re-layouts: 9.51 us -> none  [sweep_blocks(): own_index = own_slots[index]]
    dot_general x8 -> x0, matrix products: 9.21 us -> none  [the longest x4 6.64 us: score_tile(): jnp.dot(user_rows, item_block.T, precision=lax.Precision.HIGHEST, preferr...]
  transfers between devices with their start and end apart: 1 -> 0, of which waited for: 1 -> 0; matrix products, arithmetic and copies ran while one was open for 0% -> 0% of each run, Pallas kernels for 0% -> 0%
where the time goes in v1:
time: 31.7 us; the launch traced here: 31.5 us
  Pallas kernels  27.1 us (85%)
  other arithmetic  2.53 us (8%)
  local copies, waits for them, and re-layouts  1.23 us (4%)
  between operations  0.67 us (2%)
    pallas_call x1, Pallas kernels, local(): pl.pallas_call(functools.partial(kernel, n, chunks), out_shape=(jax.Shape...  27.1 us
    sub x1, other arithmetic, local(): return users - scale[0, 0] * gradient  2.53 us
    slice x1, local copies, waits for them, and re-layouts, local(): return users - scale[0, 0] * gradient  1.23 us

profile of v1, /device:TPU:0, one launch (start us, length us, event | category | flops | bytes accessed | tf_op | source)
XLA Modules:
  0.0 31.5 jit_solution(13067273707756239534)
XLA Ops:
  0.7 0.0 copy-start
  0.7 27.1 %gather_gradient.1 = (f32[256,512]{1,0:T(8,128)}, f32[8,128]{1,0:T(8,128)}) custom-call(f32[256,512]{1,0:T(8,128)} %users_hbm.1, bf16[128,512]{1,0:T(8,128)(2,1)} %items_hbm.1, s32[1,8]{1,0:T(1,128)} %blocks_ref.1, s32[1]{0:T(128)S(6)} %copy.6.count_ref, s32[256,1024]{1,0:T(8,128)} %labels_hbm.1), custom_call_target="tpu_custom_call" | custom-call | tf_op jit(solution)/shard_map/gather_gradient/pallas_call | solution.py:264
  27.8 1.2 %slice.3 = f32[1,1]{1,0:T(1,128)} slice(f32[8,128]{1,0:T(8,128)} %get-tuple-element.7), slice={[0:1], [0:1]} | slice | bytes 8 | tf_op jit(solution)/shard_map/slice | solution.py:292
  29.0 0.0 copy-done
  29.0 2.5 %multiply_subtract_fusion = f32[256,512]{1,0:T(8,128)} fusion(f32[256,512]{1,0:T(8,128)S(1)} %copy-done, f32[256,512]{1,0:T(8,128)} %get-tuple-element.8, f32[]{:T(128)} %bitcast), kind=kLoop, calls=%fused_computation | loop fusion | flops 262144 | bytes 1572868 | tf_op jit(solution)/shard_map/sub | solution.py:292
Async XLA Ops:
  0.7 28.3 %copy-start = (f32[256,512]{1,0:T(8,128)S(1)}, f32[256,512]{1,0:T(8,128)}, u32[]{:S(2)}) copy-start(f32[256,512]{1,0:T(8,128)} %users_hbm.1) | copy-start | bytes 1572868

commit v2 on v1

--- a/solution.py
+++ b/solution.py
@@ -83,8 +83,18 @@
     pl.semaphore_wait(barrier, 3)
     load_items.wait()
 
+    known = {}
+
     def chip_of(d, s):
-        return chip_near(s * (2 * d - 1))
+        if not isinstance(s, int):
+            return chip_near(s * (2 * d - 1))
+        if (d, s) not in known:
+            known[d, s] = chip_near(s * (2 * d - 1))
+        return known[d, s]
+
+    for s in {0, 1, 2, half - 2, half - 1, half} | (set(range(half)) if half <= 4 else set()):
+        for d in (0, 1):
+            chip_of(d, s)
 
     def ring_copy(d, hop, j, source):
         block = chip_of(d, source) * 2 + core
@@ -196,10 +206,11 @@
         lax.fori_loop(2, half - 1, lambda s, c: (full_step(s, False, False), c)[1], 0)
     if half > 2:
         full_step(half - 1, True, False)
-    for d, j in last:
+    earlier(half - 1, 0)
+    for i, (d, j) in enumerate(last):
         arrive(half, d, j, False)
-    earlier(half - 1, 0)
-    earlier(half - 1, 1)
+        if i == len(last) // 2 - 1:
+            earlier(half - 1, 1)
     for d in (0, 1):
         take_pair(d, half, shared(d))
     compute(chip_of(0, half))
@@ -247,7 +258,7 @@
     whole = jnp.sum(jnp.sum(whole, axis=1, keepdims=True), axis=0, keepdims=True)
     entries = height * n * users_hbm.shape[1]
     rms = jnp.sqrt(whole / entries + 1e-06)
-    scale_ref[...] = jnp.broadcast_to(0.5 / rms, scale_ref.shape)
+    scale_ref[...] = 0.5 / rms
 
 
 def solution(mesh):
@@ -259,13 +270,16 @@
         half = n // 4
         chunks = 4 if half <= 4 else 2
         dma = pltpu.SemaphoreType.DMA
+        scratch = 4 * height * (3 * width + labels.shape[1]) + 2 * n * depth * width
+        grant = 58 * 1024 * 1024
         anywhere = pl.BlockSpec(memory_space=pl.ANY)
+        far = pl.BlockSpec(memory_space=pltpu.HBM)
         scalars = pl.BlockSpec(memory_space=pltpu.SMEM)
         gradient, scale = pl.pallas_call(
             functools.partial(kernel, n, chunks),
             out_shape=(jax.ShapeDtypeStruct((height, width), jnp.float32),
-                       jax.ShapeDtypeStruct((8, 128), jnp.float32)),
-            in_specs=[anywhere, anywhere, scalars, scalars, anywhere],
+                       jax.ShapeDtypeStruct((1, 1), jnp.float32)),
+            in_specs=[far, far, scalars, scalars, far],
             out_specs=(anywhere, pl.BlockSpec(memory_space=pltpu.VMEM)),
             scratch_shapes=[
                 pltpu.VMEM((height, width), jnp.float32),
@@ -286,7 +300,7 @@
                 dma(()),
             ],
             compiler_params=pltpu.CompilerParams(
-                collective_id=0, has_side_effects=True, vmem_limit_bytes=60 * 1024 * 1024),
+                collective_id=0, has_side_effects=True, vmem_limit_bytes=grant),
             name="gather_gradient",
         )(users, items, tile_blocks, tile_count, labels)
         return users - scale[0, 0] * gradient

time: 31.7 us -> 30.4 us (0.959)
  local copies, waits for them, and re-layouts: 1.23 us -> 0.01 us
    slice x1 -> x0, local copies, waits for them, and re-layouts: 1.23 us -> none  [local(): return users - scale[0, 0] * gradient]
where the time goes in v2:
time: 30.4 us; the launch traced here: 30.2 us
  Pallas kernels  27 us (89%)
  other arithmetic  2.56 us (8%)
  between operations  0.68 us (2%)
    pallas_call x1, Pallas kernels, local(): pl.pallas_call(functools.partial(kernel, n, chunks), out_shape=(jax.Shape...  27 us
    sub x1, other arithmetic, local(): return users - scale[0, 0] * gradient  2.56 us

profile of v2, /device:TPU:0, one launch (start us, length us, event | category | flops | bytes accessed | tf_op | source)
XLA Modules:
  0.0 30.2 jit_solution(496329790559657528)
XLA Ops:
  0.7 0.0 copy-start
  0.7 27.0 %gather_gradient.1 = (f32[256,512]{1,0:T(8,128)}, f32[1,1]{1,0:T(1,128)}) custom-call(f32[256,512]{1,0:T(8,128)} %users_hbm.1, bf16[128,512]{1,0:T(8,128)(2,1)} %items_hbm.1, s32[1,8]{1,0:T(1,128)} %blocks_ref.1, s32[1]{0:T(128)S(6)} %copy.6.count_ref, s32[256,1024]{1,0:T(8,128)} %labels_hbm.1), custom_call_target="tpu_custom_call" | custom-call | tf_op jit(solution)/shard_map/gather_gradient/pallas_call | solution.py:278
  27.6 0.0 copy-done
  27.6 2.6 %multiply_subtract_fusion = f32[256,512]{1,0:T(8,128)} fusion(f32[256,512]{1,0:T(8,128)S(1)} %copy-done, f32[256,512]{1,0:T(8,128)} %get-tuple-element.8, f32[]{:T(128)} %bitcast), kind=kLoop, calls=%fused_computation | loop fusion | flops 262144 | bytes 1572868 | tf_op jit(solution)/shard_map/sub | solution.py:306
Async XLA Ops:
  0.7 27.0 %copy-start = (f32[256,512]{1,0:T(8,128)S(1)}, f32[256,512]{1,0:T(8,128)}, u32[]{:S(2)}) copy-start(f32[256,512]{1,0:T(8,128)} %users_hbm.1) | copy-start | bytes 1572868

commit v3 on v2

--- a/solution.py
+++ b/solution.py
@@ -40,7 +40,7 @@
     return there * out + (1 - there) * home
 
 
-def kernel(n, chunks, users_hbm, items_hbm, blocks_ref, count_ref, labels_hbm, grad_hbm, scale_ref,
+def kernel(n, chunks, users_hbm, items_hbm, blocks_ref, count_ref, labels_hbm, grad_hbm,
            users, labels, held, split, grad, mine, parts,
            load_sem, label_sem, ring_send, ring_recv, pair_send, pair_recv, own_sem, sum_sem, store_sem):
     chips = n // 2
@@ -220,7 +220,7 @@
     total = squares[:, 0:lanes]
     for k in range(1, squares.shape[1] // lanes):
         total = total + squares[:, k * lanes:(k + 1) * lanes]
-    total = jnp.sum(total.reshape(height // 8, 8, lanes), axis=0)
+    total = jnp.sum(jnp.sum(total.reshape(height // 8, 8, lanes), axis=0), axis=0, keepdims=True)
     mine[...] = total
 
     def sum_copy(k):
@@ -233,8 +233,6 @@
             sum_copy(k).start()
     else:
         lax.fori_loop(1, n, lambda k, c: (sum_copy(k).start(), c)[1], 0)
-    store = pltpu.make_async_copy(grad, grad_hbm, store_sem)
-    store.start()
 
     own_copy(me).wait_send()
 
@@ -250,7 +248,6 @@
     else:
         lax.fori_loop(1, half, lambda s, c: (drain(s, order, order), c)[1], 0)
     drain(half, last, last)
-    store.wait()
 
     pltpu.make_async_copy(parts, parts, sum_sem.at[1]).wait()
     pltpu.make_async_copy(parts, parts, sum_sem.at[0]).wait()
@@ -258,7 +255,10 @@
     whole = jnp.sum(jnp.sum(whole, axis=1, keepdims=True), axis=0, keepdims=True)
     entries = height * n * users_hbm.shape[1]
     rms = jnp.sqrt(whole / entries + 1e-06)
-    scale_ref[...] = 0.5 / rms
+    grad[...] = users[...] - (0.5 / rms) * grad[...]
+    store = pltpu.make_async_copy(grad, grad_hbm, store_sem)
+    store.start()
+    store.wait()
 
 
 def solution(mesh):
@@ -275,20 +275,19 @@
         anywhere = pl.BlockSpec(memory_space=pl.ANY)
         far = pl.BlockSpec(memory_space=pltpu.HBM)
         scalars = pl.BlockSpec(memory_space=pltpu.SMEM)
-        gradient, scale = pl.pallas_call(
+        return pl.pallas_call(
             functools.partial(kernel, n, chunks),
-            out_shape=(jax.ShapeDtypeStruct((height, width), jnp.float32),
-                       jax.ShapeDtypeStruct((1, 1), jnp.float32)),
+            out_shape=jax.ShapeDtypeStruct((height, width), jnp.float32),
             in_specs=[far, far, scalars, scalars, far],
-            out_specs=(anywhere, pl.BlockSpec(memory_space=pltpu.VMEM)),
+            out_specs=anywhere,
             scratch_shapes=[
                 pltpu.VMEM((height, width), jnp.float32),
                 pltpu.VMEM((tile_blocks.shape[1], height, depth), jnp.int32),
                 pltpu.VMEM((n * depth, width), jnp.bfloat16),
                 pltpu.VMEM((2 * height, width), jnp.bfloat16),
                 pltpu.VMEM((height, width), jnp.float32),
-                pltpu.VMEM((8, 128), jnp.float32),
-                pltpu.VMEM((n - 1, 8, 128), jnp.float32),
+                pltpu.VMEM((1, 128), jnp.float32),
+                pltpu.VMEM((n - 1, 1, 128), jnp.float32),
                 dma((2,)),
                 dma((tile_blocks.shape[1],)),
                 dma((2, half, chunks)),
@@ -303,7 +302,6 @@
                 collective_id=0, has_side_effects=True, vmem_limit_bytes=grant),
             name="gather_gradient",
         )(users, items, tile_blocks, tile_count, labels)
-        return users - scale[0, 0] * gradient
 
     rows = P(("group", "loop"), None)
     return jax.shard_map(local, mesh=mesh, in_specs=(rows, rows, rows, P(("group", "loop")), rows),

time: 30.4 us -> 29.7 us (0.977)
  other arithmetic: 2.56 us -> 0 us
  local copies, waits for them, and re-layouts: 0.01 us -> 1.87 us
    sub x1 -> x0, other arithmetic: 2.56 us -> none  [local(): return users - scale[0, 0] * gradient]
    unnamed x2 -> x1, local copies, waits for them, and re-layouts: 0.01 us -> 1.87 us
where the time goes in v3:
time: 29.7 us; the launch traced here: 29.5 us
  Pallas kernels  27 us (91%)
  local copies, waits for them, and re-layouts  1.87 us (6%)
  between operations  0.66 us (2%)
    pallas_call x1, Pallas kernels, local(): pl.pallas_call(functools.partial(kernel, n, chunks), out_shape=jax.ShapeD...  27 us
    unnamed x1, local copies, waits for them, and re-layouts  1.87 us

profile of v3, /device:TPU:0, one launch (start us, length us, event | category | flops | bytes accessed | tf_op | source)
XLA Modules:
  0.0 29.5 jit_solution(9895608025833547724)
XLA Ops:
  0.7 27.0 %gather_gradient.1 = f32[256,512]{1,0:T(8,128)} custom-call(f32[256,512]{1,0:T(8,128)} %users_hbm.1, bf16[128,512]{1,0:T(8,128)(2,1)} %items_hbm.1, s32[1,8]{1,0:T(1,128)} %blocks_ref.1, s32[1]{0:T(128)S(6)} %copy.7.count_ref, s32[256,1024]{1,0:T(8,128)} %labels_hbm.1), custom_call_target="tpu_custom_call" | custom-call | tf_op jit(solution)/shard_map/gather_gradient/pallas_call | solution.py:278
  27.6 1.9 %copy.8 = f32[256,512]{1,0:T(8,128)} copy(f32[256,512]{1,0:T(8,128)} %gather_gradient.1) | data formatting | bytes 1048576

commit v4 on v3

--- a/solution.py
+++ b/solution.py
@@ -206,11 +206,11 @@
         lax.fori_loop(2, half - 1, lambda s, c: (full_step(s, False, False), c)[1], 0)
     if half > 2:
         full_step(half - 1, True, False)
-    earlier(half - 1, 0)
     for i, (d, j) in enumerate(last):
         arrive(half, d, j, False)
         if i == len(last) // 2 - 1:
-            earlier(half - 1, 1)
+            earlier(half - 1, 0)
+    earlier(half - 1, 1)
     for d in (0, 1):
         take_pair(d, half, shared(d))
     compute(chip_of(0, half))

time: 29.7 us -> 29.2 us (0.983)
  Pallas kernels: 27 us -> 26.5 us
    pallas_call x1, Pallas kernels: 27 us -> 26.5 us  [local(): pl.pallas_call(functools.partial(kernel, n, chunks), out_shape=jax.ShapeD...]
where the time goes in v4:
time: 29.2 us; the launch traced here: 29 us
  Pallas kernels  26.5 us (91%)
  local copies, waits for them, and re-layouts  1.87 us (6%)
  between operations  0.66 us (2%)
    pallas_call x1, Pallas kernels, local(): pl.pallas_call(functools.partial(kernel, n, chunks), out_shape=jax.ShapeD...  26.5 us
    unnamed x1, local copies, waits for them, and re-layouts  1.87 us

profile of v4, /device:TPU:0, one launch (start us, length us, event | category | flops | bytes accessed | tf_op | source)
XLA Modules:
  0.0 29.0 jit_solution(10236460340890428826)
XLA Ops:
  0.7 26.5 %gather_gradient.1 = f32[256,512]{1,0:T(8,128)} custom-call(f32[256,512]{1,0:T(8,128)} %users_hbm.1, bf16[128,512]{1,0:T(8,128)(2,1)} %items_hbm.1, s32[1,8]{1,0:T(1,128)} %blocks_ref.1, s32[1]{0:T(128)S(6)} %copy.7.count_ref, s32[256,1024]{1,0:T(8,128)} %labels_hbm.1), custom_call_target="tpu_custom_call" | custom-call | tf_op jit(solution)/shard_map/gather_gradient/pallas_call | solution.py:278
  27.1 1.9 %copy.8 = f32[256,512]{1,0:T(8,128)} copy(f32[256,512]{1,0:T(8,128)} %gather_gradient.1) | data formatting | bytes 1048576
